TPU v7x, 32 devices: a whole 2x2x4 slice. The times are simulated.
32 devices in a mesh: row: 8 (over y, x, core), col: 4 (over z).
Axes of the slice: x: 2, y: 2, z: 4, core: 2. Of those that a mesh axis runs over, the one named last changes fastest.
Arguments:
- inverse: float32 [20480, 20480], P('row', 'col'), may hold values from -6 to 6
- factor: float32 [20480, 2, 256], P(('row', 'col')), may hold values from -0.0390625 to 0.0390625
- diag_inverse: float32 [2, 256, 256], replicated, may hold values from -6 to 6
- block_sizes: int32 [64], replicated, may hold values from 1 to 1280, 20480 in all
- listed: int32 [2, 64], replicated, may hold values 0 or 1
Outputs:
- ancestor_rows: float32 [20480, 2, 256], P(('row', 'col'))
- diagonal_block: float32 [2, 256, 256], replicated
Inputs may be any that keep to these rules, and one draw needn't show every extreme that they name: `block_sizes`: positive sizes that sum to 20480; the largest is exactly 1280.
All inputs are finite; a program needn't handle non-finite values.
Results may differ from a plain program's by a relative error of at most 0.00007.
Values sent between devices are 32-bit elements; how exact they have to be, the bound alone decides.
A program may use at most 128 MiB of HBM per device.

v0:
```python
import jax
import jax.numpy as jnp
from jax import lax
from jax.sharding import PartitionSpec as P


def from_root(value, axis, source):
    kept = jnp.where(lax.axis_index(axis) == source, value, 0).astype(value.dtype)
    return lax.psum(kept, axis)


def membership(first_row, row_total, block_sizes, listed):
    block_ends = jnp.cumsum(block_sizes)
    block_starts = block_ends - block_sizes
    positions = first_row + jnp.arange(row_total, dtype=jnp.int32)
    inside = (
        (positions[:, None] >= block_starts[None, :]) & (positions[:, None] < block_ends[None, :])
    ).astype(jnp.float32)
    return jnp.dot(
        inside,
        listed.astype(jnp.float32).T,
        precision=lax.Precision.HIGHEST,
        preferred_element_type=jnp.float32,
    )


def per_device(inverse, factor, diag_inverse, block_sizes, listed):
    n_rowdev = lax.axis_size("row")
    n_coldev = lax.axis_size("col")
    row_place = lax.axis_index("row")
    col_place = lax.axis_index("col")
    shard_rows = factor.shape[0]
    sibling_count = factor.shape[1]
    width = factor.shape[2]
    ratio = n_rowdev // n_coldev
    row_block = lax.all_gather(factor, "col", axis=0, tiled=True)
    gathered = []
    for offset in range(ratio):
        gathered.append(from_root(row_block, "row", col_place * ratio + offset))
    col_block = jnp.concatenate(gathered, axis=0)
    col_rows = col_block.shape[0]
    col_member = membership(col_place * col_rows, col_rows, block_sizes, listed)
    panel = (col_block * col_member[:, :, None]).reshape(col_rows, sibling_count * width)
    block_total = inverse.shape[0]
    partial_value = -jnp.dot(
        inverse, panel, precision=lax.Precision.HIGHEST, preferred_element_type=jnp.float32
    )
    summed = lax.psum(partial_value, "col")
    block_member = membership(row_place * block_total, block_total, block_sizes, listed)
    block_result = summed.reshape(block_total, sibling_count, width) * block_member[:, :, None]
    schur_term = jnp.einsum(
        "isw,isv->swv", row_block, block_result, precision=lax.Precision.HIGHEST
    )
    schur = lax.psum(schur_term, "row")
    ancestor_rows = lax.dynamic_slice_in_dim(block_result, col_place * shard_rows, shard_rows, 0)
    return (ancestor_rows, diag_inverse - schur)


def solution(mesh):
    in_specs = (P("row", "col"), P(("row", "col"), None, None), P(), P(), P())
    out_specs = (P(("row", "col"), None, None), P())
    return jax.shard_map(
        per_device, mesh=mesh, in_specs=in_specs, out_specs=out_specs, check_vma=False
    )
```

profile of v0, /device:TPU:0, one launch (start us, length us, event | category | flops | bytes accessed | tf_op | source)
XLA Modules:
  0.0 653.9 jit_solution(9232629267015286627)
XLA Ops:
  7.2 2.5 copy.24
  9.8 101.1 %all-gather.2.cloned.1.call-done = f32[2560,2,256]{2,0,1:T(8,128)} async-done(((f32[640,2,256]{2,0,1:T(8,128)}), f32[2560,2,256]{2,0,1:T(8,128)}) %all-gather.2.cloned.1.call-update) | async-done | bytes 5242896 | tf_op jit(solution)/shard_map/all_gather | solution.py:36
  110.9 7.2 %broadcast_select_fusion.1 = (f32[2560,2,256]{2,0,1:T(8,128)}, f32[2560,2,256]{2,0,1:T(8,128)}) fusion(f32[2560,2,256]{2,0,1:T(8,128)} %all-gather.2.cloned.1.call-done, pred[]{:T(512)S(6)} %eq.6, pred[]{:T(512)S(6)} %eq.7), kind=kLoop, calls=%fused_computation.9 | loop fusion | flops 2621440 | bytes 15728642 | tf_op jit(solution)/shard_map/jit(_where)/select_n | solution.py:8
  118.1 5.9 copy.25
  124.0 5.9 copy.26
  130.0 0.6 copy-done.3
  130.6 0.1 copy.27
  130.8 0.1 reduce
  130.9 0.6 fusion.10
  131.6 146.0 %all-reduce.9.cloned.1.call-done = (f32[2560,512]{0,1:T(8,128)}, f32[2560,512]{0,1:T(8,128)}) async-done(((f32[2560,512]{0,1:T(8,128)}, f32[2560,512]{0,1:T(8,128)}), (f32[2560,512]{0,1:T(8,128)}, f32[2560,512]{0,1:T(8,128)})) %all-reduce.9.cloned.1.call-update) | async-done | bytes 10485776 | tf_op jit(solution)/shard_map/psum | solution.py:9
  277.5 5.2 mul.34
  282.8 91.4 %fusion.5 = f32[512,2560]{1,0:T(8,128)} fusion(f32[2560,5120]{1,0:T(8,128)} %param.5, f32[5120,512]{0,1:T(8,128)} %bitcast.14, f32[2560,512]{0,1:T(8,128)} %get-tuple-element.8, f32[2560,512]{0,1:T(8,128)} %get-tuple-element.9), kind=kOutput, calls=%fused_computation.6 | convolution fusion | flops 80537190400 | bytes 78643200 | tf_op jit(solution)/shard_map/dot_general | solution.py:45
  374.2 8.7 %copy.28 = f32[2560,2,256]{2,1,0:T(2,128)} copy(f32[2560,2,256]{0,2,1:T(8,128)} %bitcast.15) | data formatting | bytes 10485760 | tf_op jit(solution)/shard_map/reshape | solution.py:50
  382.9 0.2 all-reduce.7.cloned.1.call-start
  383.2 0.9 fusion.6
  384.0 188.0 %all-reduce.5.cloned.1.call-done = f32[2560,2,256]{2,1,0:T(2,128)} async-done(((f32[2560,2,256]{2,1,0:T(2,128)}), f32[2560,2,256]{2,1,0:T(2,128)}) %all-reduce.5.cloned.1.call-update) | async-done | bytes 5242896 | tf_op jit(solution)/shard_map/psum | solution.py:48
  572.1 5.5 broadcast_multiply_fusion
  577.6 2.3 copy-done
  579.9 11.5 %fusion.11 = f32[2,256,256]{1,2,0:T(8,128)} fusion(f32[2560,2,256]{2,0,1:T(8,128)} %all-gather.2.cloned.1.call-done, f32[2560,2,256]{2,1,0:T(2,128)S(1)} %broadcast_multiply_fusion), kind=kOutput, calls=%fused_computation.16 | convolution fusion | flops 4026531840 | bytes 11010048 | tf_op jit(solution)/shard_map/isw,isv->swv/dot_general | solution.py:51
  591.4 0.2 copy.31
  591.6 2.8 constant_dynamic-slice_fusion
  594.4 50.8 %all-reduce.7.cloned.1.call-done = f32[2,256,256]{1,2,0:T(8,128)} async-done(((f32[2,256,256]{1,2,0:T(8,128)}), f32[2,256,256]{1,2,0:T(8,128)}) %all-reduce.7.cloned.1.call-update) | async-done | bytes 524304 | tf_op jit(solution)/shard_map/psum | solution.py:54
  645.3 1.1 sub.8
  646.4 1.0 copy.32
  (17 shorter events, 0.3 us)
Async XLA Ops:
  7.2 103.7 %all-gather.2.cloned.1.call-start = ((), (), s32[]{:S(2)}) async-start(), calls=%async_computation | async-start | bytes 6553600 | tf_op jit(solution)/shard_map/all_gather | solution.py:36
  9.7 267.8 %all-reduce.9.cloned.1.call-start = ((), (), s32[]{:S(2)}) async-start(), calls=%async_computation.3 | async-start | bytes 20971520 | tf_op jit(solution)/shard_map/psum | solution.py:9
  129.9 0.7 copy-start.3
  129.9 1.0 copy-start.2
  130.0 442.1 %all-reduce.5.cloned.1.call-start = ((), (), s32[]{:S(2)}) async-start(), calls=%async_computation.1 | async-start | bytes 10485760 | tf_op jit(solution)/shard_map/psum | solution.py:48
  382.9 262.4 %all-reduce.7.cloned.1.call-start = ((), (), s32[]{:S(2)}) async-start(), calls=%async_computation.2 | async-start | bytes 1048576 | tf_op jit(solution)/shard_map/psum | solution.py:54
  577.6 2.3 copy-start
  579.9 11.5 %copy-start.1 = (f32[2,256,256]{2,1,0:T(8,128)S(1)}, f32[2,256,256]{2,1,0:T(8,128)}, u32[]{:S(2)}) copy-start(f32[2,256,256]{2,1,0:T(8,128)} %param.7) | copy-start | bytes 1572868
Sparse Core Ops, SparseCore 0:
  10.1 100.7 all-gather.1
  130.1 147.3 all-reduce.8
  383.0 188.9 all-reduce.4
  591.5 53.7 all-reduce.6
where the time goes:
time: 655 us; the launch traced here: 654 us
  waiting for transfers between devices  486 us (74%)
  matrix products  104 us (16%)
  local copies, waits for them, and re-layouts  35.2 us (5%)
  other arithmetic  14.1 us (2%)
  between operations  13.9 us (2%)
    psum x1, waiting for transfers between devices, per_device(): summed = lax.psum(partial_value, 'col')  188 us
    psum x1, waiting for transfers between devices, from_root(): return lax.psum(kept, axis)  146 us
    all_gather x1, waiting for transfers between devices, per_device(): row_block = lax.all_gather(factor, 'col', axis=0, tiled=True)  101 us
    dot_general x1, matrix products, per_device(): jnp.dot(inverse, panel, precision=lax.Precision.HIGHEST, preferred_elemen...  91.4 us
    psum x1, waiting for transfers between devices, per_device(): schur = lax.psum(schur_term, 'row')  50.8 us
  transfers between devices with their start and end apart: 4, of which 4 were waited for; matrix products, arithmetic and copies ran while one was open for 1% of the time, Pallas kernels for 0%

commit v1 on v0

--- a/solution.py
+++ b/solution.py
@@ -45,7 +45,9 @@
     partial_value = -jnp.dot(
         inverse, panel, precision=lax.Precision.HIGHEST, preferred_element_type=jnp.float32
     )
-    summed = lax.psum(partial_value, "col")
+    summed = partial_value
+    for hop in (1, 2):
+        summed = summed + lax.ppermute(summed, "col", [(dev, dev ^ hop) for dev in range(4)])
     block_member = membership(row_place * block_total, block_total, block_sizes, listed)
     block_result = summed.reshape(block_total, sibling_count, width) * block_member[:, :, None]
     schur_term = jnp.einsum(

time: 655 us -> 820 us (1.25)
  waiting for transfers between devices: 486 us -> 637 us
  other arithmetic: 14.1 us -> 27.4 us
    ppermute x0 -> x2, waiting for transfers between devices: none -> 337 us  [per_device(): lax.ppermute(summed, 'col', [(dev, dev ^ hop) for dev in range(4)])]
    psum x1 -> x0, waiting for transfers between devices: 188 us -> none  [per_device(): summed = lax.psum(partial_value, 'col')]
    add x0 -> x2, other arithmetic: none -> 13.2 us  [per_device(): summed + lax.ppermute(summed, 'col', [(dev, dev ^ hop) for dev in range(4)])]
  transfers between devices with their start and end apart: 4 -> 5, of which waited for: 4 -> 5; matrix products, arithmetic and copies ran while one was open for 1% -> 1% of each run, Pallas kernels for 0% -> 0%
where the time goes in v1:
time: 820 us; the launch traced here: 819 us
  waiting for transfers between devices  637 us (78%)
  matrix products  102 us (12%)
  local copies, waits for them, and re-layouts  35.4 us (4%)
  other arithmetic  27.4 us (3%)
  between operations  13.9 us (2%)
    ppermute x2, waiting for transfers between devices, per_device(): lax.ppermute(summed, 'col', [(dev, dev ^ hop) for dev in range(4)])  337 us
    psum x1, waiting for transfers between devices, from_root(): return lax.psum(kept, axis)  146 us
    all_gather x1, waiting for transfers between devices, per_device(): row_block = lax.all_gather(factor, 'col', axis=0, tiled=True)  101 us
    dot_general x1, matrix products, per_device(): jnp.dot(inverse, panel, precision=lax.Precision.HIGHEST, preferred_elemen...  91.4 us
    psum x1, waiting for transfers between devices, per_device(): schur = lax.psum(schur_term, 'row')  52.3 us
  transfers between devices with their start and end apart: 5, of which 5 were waited for; matrix products, arithmetic and copies ran while one was open for 1% of the time, Pallas kernels for 0%

profile of v1, /device:TPU:0, one launch (start us, length us, event | category | flops | bytes accessed | tf_op | source)
XLA Modules:
  0.0 819.5 jit_solution(10184631163930240483)
XLA Ops:
  7.2 2.5 copy.24
  9.8 101.1 %all-gather.2.cloned.1.call-done = f32[2560,2,256]{2,0,1:T(8,128)} async-done(((f32[640,2,256]{2,0,1:T(8,128)}), f32[2560,2,256]{2,0,1:T(8,128)}) %all-gather.2.cloned.1.call-update) | async-done | bytes 5242896 | tf_op jit(solution)/shard_map/all_gather | solution.py:36
  110.9 7.2 broadcast_select_fusion.1
  118.1 5.9 copy.25
  124.0 5.9 copy.26
  131.0 0.6 fusion.9
  131.6 146.0 %all-reduce.6.cloned.1.call-done = (f32[2560,512]{0,1:T(8,128)}, f32[2560,512]{0,1:T(8,128)}) async-done(((f32[2560,512]{0,1:T(8,128)}, f32[2560,512]{0,1:T(8,128)}), (f32[2560,512]{0,1:T(8,128)}, f32[2560,512]{0,1:T(8,128)})) %all-reduce.6.cloned.1.call-update) | async-done | bytes 10485776 | tf_op jit(solution)/shard_map/psum | solution.py:9
  277.6 5.2 mul.34
  282.8 91.4 %negate_bitcast_fusion = f32[2560,512]{0,1:T(8,128)} fusion(f32[2560,5120]{1,0:T(8,128)} %param.5, f32[5120,512]{0,1:T(8,128)} %bitcast.18, f32[2560,512]{0,1:T(8,128)} %get-tuple-element.8, f32[2560,512]{0,1:T(8,128)} %get-tuple-element.9), kind=kOutput, calls=%fused_computation.6 | convolution fusion | flops 80537190400 | bytes 78643200 | tf_op jit(solution)/shard_map/dot_general | solution.py:45
  374.2 1.5 collective-permute-start
  375.7 113.2 %collective-permute-done = f32[2560,512]{0,1:T(8,128)S(1)} collective-permute-done((f32[2560,512]{0,1:T(8,128)}, f32[2560,512]{0,1:T(8,128)S(1)}, u32[]{:S(2)}, u32[]{:S(2)}) %collective-permute-start) | collective-permute-done | bytes 5242912 | tf_op jit(solution)/shard_map/ppermute | solution.py:50
  488.9 5.8 add.41
  494.8 2.4 collective-permute-start.1
  497.2 0.9 fusion.5
  498.0 223.9 %collective-permute-done.1 = f32[2560,512]{0,1:T(8,128)} collective-permute-done((f32[2560,512]{0,1:T(8,128)}, f32[2560,512]{0,1:T(8,128)}, u32[]{:S(2)}, u32[]{:S(2)}) %collective-permute-start.1) | collective-permute-done | bytes 5242912 | tf_op jit(solution)/shard_map/ppermute | solution.py:50
  722.0 7.4 add.42
  729.4 8.8 %copy.29 = f32[2560,2,256]{2,1,0:T(2,128)} copy(f32[2560,2,256]{0,2,1:T(8,128)} %bitcast.17) | data formatting | bytes 10485760 | tf_op jit(solution)/shard_map/reshape | solution.py:52
  738.2 5.7 broadcast_multiply_fusion
  743.9 2.3 copy-done
  746.2 9.2 %fusion.10 = f32[2,256,256]{1,2,0:T(8,128)} fusion(f32[2560,2,256]{2,0,1:T(8,128)S(1)} %bitcast.14, f32[2560,2,256]{2,1,0:T(2,128)S(1)} %broadcast_multiply_fusion), kind=kOutput, calls=%fused_computation.16 | convolution fusion | flops 4026531840 | bytes 11010048 | tf_op jit(solution)/shard_map/isw,isv->swv/dot_general | solution.py:53
  755.7 2.8 constant_dynamic-slice_fusion
  758.5 52.3 %all-reduce.4.cloned.1.call-done = f32[2,256,256]{1,2,0:T(8,128)} async-done(((f32[2,256,256]{1,2,0:T(8,128)}), f32[2,256,256]{1,2,0:T(8,128)}) %all-reduce.4.cloned.1.call-update) | async-done | bytes 524304 | tf_op jit(solution)/shard_map/psum | solution.py:56
  810.8 1.1 sub.8
  812.0 1.0 copy.32
  (25 shorter events, 1.3 us)
Async XLA Ops:
  7.2 103.7 %all-gather.2.cloned.1.call-start = ((), (), s32[]{:S(2)}) async-start(), calls=%async_computation | async-start | bytes 6553600 | tf_op jit(solution)/shard_map/all_gather | solution.py:36
  9.7 267.9 %all-reduce.6.cloned.1.call-start = ((), (), s32[]{:S(2)}) async-start(), calls=%async_computation.2 | async-start | bytes 20971520 | tf_op jit(solution)/shard_map/psum | solution.py:9
  130.0 0.7 copy-start.3
  130.0 1.0 copy-start.2
  130.0 680.8 %all-reduce.4.cloned.1.call-start = ((), (), s32[]{:S(2)}) async-start(), calls=%async_computation.1 | async-start | bytes 1048576 | tf_op jit(solution)/shard_map/psum | solution.py:56
  374.2 114.7 %collective-permute-start = (f32[2560,512]{0,1:T(8,128)}, f32[2560,512]{0,1:T(8,128)S(1)}, u32[]{:S(2)}, u32[]{:S(2)}) collective-permute-start(f32[2560,512]{0,1:T(8,128)} %negate_bitcast_fusion), channel_id=1, source_target_pairs={{0,1},{1,0},{2,3},{3,2},{4,5},{5,4},{6,7},{7,6},{8,9},{9,8},{10,11... | collective-permute-start | bytes 15728648 | tf_op jit(solution)/shard_map/ppermute | solution.py:50
  494.8 227.2 %collective-permute-start.1 = (f32[2560,512]{0,1:T(8,128)}, f32[2560,512]{0,1:T(8,128)}, u32[]{:S(2)}, u32[]{:S(2)}) collective-permute-start(f32[2560,512]{0,1:T(8,128)} %add.41), channel_id=1, source_target_pairs={{0,2},{1,3},{2,0},{3,1},{4,6},{5,7},{6,4},{7,5},{8,10},{9,11},{10,... | collective-permute-start | bytes 15728648 | tf_op jit(solution)/shard_map/ppermute | solution.py:50
  729.4 16.8 %slice-start = ((s8[5242880]{0:T(1024)(128)(4,1)}), s8[1048576]{0:T(1024)(128)(4,1)S(1)}, s32[]{:S(2)}) async-start(s8[5242880]{0:T(1024)(128)(4,1)} %bitcast.13), calls=%async_computation.3 | async-start | bytes 2097152
  738.2 8.0 slice-start.1
  743.9 2.3 copy-start
  746.2 9.3 %copy-start.1 = (f32[2,256,256]{2,1,0:T(8,128)S(1)}, f32[2,256,256]{2,1,0:T(8,128)}, u32[]{:S(2)}) copy-start(f32[2,256,256]{2,1,0:T(8,128)} %param.7) | copy-start | bytes 1572868
Sparse Core Ops, SparseCore 0:
  10.1 100.7 all-gather.1
  130.1 147.3 all-reduce.5
  755.6 55.2 all-reduce.3
